TPU v7x, 32 devices: a whole 2x2x4 slice. The times are simulated.
32 devices in a mesh: seg: 2 (over x), genome: 16 (over z, y, core).
Axes of the slice: x: 2, y: 2, z: 4, core: 2. Of those that a mesh axis runs over, the one named last changes fastest.
Arguments:
- z_typed: float32 [256, 16384], P(None, ('seg', 'genome')), parts along dimension 1, may hold values from -8 to 8
- diag_inverse: float32 [32, 512, 512], P(('seg', 'genome')), parts along dimension 0
- coupling: float32 [32, 512, 256], P(('seg', 'genome')), parts along dimension 0
- impute_coef: bfloat16 [16384, 1024], P(('seg', 'genome')), parts along dimension 0, may hold values from -0.25 to 0.25
- anchor: int32 [16384], P(('seg', 'genome')), parts along dimension 0, may hold values from 0 to 8191, as said below
Outputs:
- imputed: float32 [256, 16384], P(None, ('seg', 'genome')), parts along dimension 1
There are 2 independent parts, one for each index of `seg`. A program takes and returns all parts, laid end to end along the dimension named above; each array names one. Nothing has to cross between parts.
Inputs may be any that keep to these rules, and one draw needn't show every extreme that they name: The anchor of the untyped variant t lies in typed block t // 512, i.e. in columns (t // 512) * 512 to (t // 512 + 1) * 512 - 1.
All inputs are finite; a program needn't handle non-finite values.
Results may differ from a plain program's by a relative error of at most 0.002.
The roundings to bfloat16 on the way count: a program that leaves them out, or rounds other values in their place, can miss the bound.
Values may be sent and summed in bfloat16 or wider, within the bound.
A program may use at most 192 MiB of HBM per device.

v0:
```python
import jax
import jax.numpy as jnp
from jax import lax
from jax.sharding import PartitionSpec as P

precise = lax.Precision.HIGHEST


def entering(part, axis, combine, identity, reverse):
    count = lax.axis_size(axis)
    place = lax.axis_index(axis)
    ahead = count - 1 - place if reverse else place
    gathered = jax.tree.map(lambda a: lax.all_gather(a, axis), part)
    state = jax.tree.map(lambda a, e: jnp.zeros_like(a) + jnp.asarray(e, a.dtype), part, identity)

    def one(step, state):
        source = count - 1 - step if reverse else step
        return combine(
            state, jax.tree.map(lambda a: lax.dynamic_index_in_dim(a, source, 0, False), gathered)
        )

    return lax.fori_loop(0, ahead, one, state)


def from_behind(block, axis, distance):
    devices = range(lax.axis_size(axis))
    route = [(i - distance, i) for i in devices if i - distance in devices]
    return lax.ppermute(block, axis, route)


def compose(earlier, later):
    return (
        jnp.dot(earlier[0], later[0], precision=precise),
        jnp.dot(earlier[1], later[0], precision=precise) + later[1],
    )


def contract(values, coefs):
    return lax.dot_general(
        values, coefs, (((1,), (1,)), ((), ())), preferred_element_type=jnp.float32
    )


def per_device(z_typed, diag_inverse, coupling, impute_coef, anchor):
    inverse_block = diag_inverse[0]
    couple = coupling[0]
    typed_len = inverse_block.shape[0]
    half_width = couple.shape[1]
    traits = z_typed.shape[0]
    projected = jnp.dot(inverse_block, couple, precision=precise)
    solved = jnp.dot(z_typed, inverse_block.T, precision=precise)
    chain_map = -projected[typed_len - half_width :, :]
    tail_source = solved[:, typed_len - half_width :]
    empty_tail = jnp.zeros((traits, half_width), jnp.float32)
    identity = (jnp.eye(half_width, dtype=jnp.float32), empty_tail)
    forward = entering((chain_map.T, tail_source), "genome", compose, identity, False)
    forward_rows = solved - jnp.dot(forward[1], projected.T, precision=precise)
    backward = entering(
        (chain_map, jnp.dot(forward_rows, projected, precision=precise)),
        "genome",
        compose,
        identity,
        True,
    )
    upper_in = backward[1]
    padded = jnp.concatenate(
        [jnp.zeros((traits, typed_len - half_width), jnp.float32), upper_in], axis=1
    )
    weights = jnp.dot(forward_rows - padded, inverse_block, precision=precise).astype(jnp.bfloat16)
    span = typed_len + 2 * half_width
    columns = lax.axis_index("genome") * typed_len - half_width + jnp.arange(span, dtype=jnp.int32)
    within = jnp.abs(columns[None, :] - anchor[:, None]) <= half_width
    masked = jnp.where(within, impute_coef, jnp.zeros_like(impute_coef))
    left_edge = from_behind(weights[:, typed_len - half_width :], "genome", 1)
    right_edge = from_behind(weights[:, :half_width], "genome", -1)
    imputed = contract(weights, masked[:, half_width : half_width + typed_len])
    imputed = imputed + contract(left_edge, masked[:, :half_width])
    imputed = imputed + contract(right_edge, masked[:, half_width + typed_len :])
    return imputed


def solution(mesh):
    in_specs = (
        P(None, ("seg", "genome")),
        P(("seg", "genome"), None, None),
        P(("seg", "genome"), None, None),
        P(("seg", "genome"), None),
        P(("seg", "genome")),
    )
    out_specs = P(None, ("seg", "genome"))
    return jax.shard_map(
        per_device, mesh=mesh, in_specs=in_specs, out_specs=out_specs, check_vma=False
    )
```

profile of v0, /device:TPU:1, one launch (start us, length us, event | category | flops | bytes accessed | tf_op | source)
XLA Modules:
  0.0 273.8 jit_solution(10322707247675112382)
XLA Ops:
  6.5 1.2 copy-done
  7.8 2.0 fusion.10
  10.7 2.1 fusion.12
  14.3 51.4 %all-gather.9.cloned.1.call-done = f32[4096,256]{0,1:T(8,128)} async-done(((f32[256,256]{0,1:T(8,128)}), f32[4096,256]{0,1:T(8,128)}) %all-gather.9.cloned.1.call-update) | async-done | bytes 4194320 | tf_op jit(solution)/shard_map/all_gather | solution.py:13
  65.8 5.6 %copy.10 = f32[4096,256]{1,0:T(8,128)} copy(f32[4096,256]{0,1:T(8,128)} %all-gather.9.cloned.1.call-done) | data formatting | bytes 8388608 | tf_op jit(solution)/shard_map/while | solution.py:22
  71.4 45.1 %all-gather.11.cloned.1.call-done = f32[4096,256]{1,0:T(8,128)} async-done(((f32[256,256]{1,0:T(8,128)}), f32[4096,256]{1,0:T(8,128)}) %all-gather.11.cloned.1.call-update) | async-done | bytes 4194320 | tf_op jit(solution)/shard_map/all_gather | solution.py:13
  116.5 2.7 while.26
  116.6 1.0 constant_dynamic-slice_fusion.4
  117.7 1.6 fusion.43
  119.3 1.0 convolution_subtract_fusion
  120.3 1.3 fusion.24
  121.7 1.8 fusion.8
  123.5 44.1 %all-gather.13.cloned.1.call-done = f32[4096,256]{1,0:T(8,128)} async-done(((f32[256,256]{1,0:T(8,128)}), f32[4096,256]{1,0:T(8,128)}) %all-gather.13.cloned.1.call-update) | async-done | bytes 4194320 | tf_op jit(solution)/shard_map/all_gather | solution.py:13
  167.6 50.9 %all-gather.15.cloned.1.call-done = f32[4096,256]{1,0:T(8,128)} async-done(((f32[256,256]{1,0:T(8,128)}), f32[4096,256]{1,0:T(8,128)}) %all-gather.15.cloned.1.call-update) | async-done | bytes 4194320 | tf_op jit(solution)/shard_map/all_gather | solution.py:13
  218.6 38.2 %while.27 = (s32[]{:T(128)}, f32[256,256]{0,1:T(8,128)S(1)}, s32[]{:T(128)}, f32[16,256,256]{2,1,0:T(8,128)}, f32[16,256,256]{2,1,0:T(8,128)}, /*index=5*/s32[]{:T(128)}, s32[]{:T(128)}, s32[]{:T(128)}, s32[]{:T(128)}) while((s32[]{:T(128)}, f32[256,256]{0,1:T(8,128)S(1)}, s32[]{:T(128)}, f32[16,256,256]{2,1,0:T(8,128)}, ...), condition=%wide.region_3.4_spmd, body=%wide.region_2.3_spmd.sunk | while | flops 201392128 | bytes 2621587 | solution.py:22
  218.6 1.0 constant_dynamic-slice_fusion.5
  219.8 1.6 fusion.46
  221.3 1.0 constant_dynamic-slice_fusion.5
  222.5 1.6 fusion.46
  224.1 1.0 constant_dynamic-slice_fusion.5
  225.2 1.6 fusion.46
  226.8 1.0 constant_dynamic-slice_fusion.5
  227.9 1.6 fusion.46
  229.5 1.0 constant_dynamic-slice_fusion.5
  230.7 1.6 fusion.46
  232.2 1.0 constant_dynamic-slice_fusion.5
  233.4 1.6 fusion.46
  235.0 1.0 constant_dynamic-slice_fusion.5
  236.1 1.6 fusion.46
  237.7 1.0 constant_dynamic-slice_fusion.5
  238.8 1.6 fusion.46
  240.4 1.0 constant_dynamic-slice_fusion.5
  241.6 1.6 fusion.46
  243.1 1.0 constant_dynamic-slice_fusion.5
  244.3 1.6 fusion.46
  245.9 1.0 constant_dynamic-slice_fusion.5
  247.0 1.6 fusion.46
  248.6 1.0 constant_dynamic-slice_fusion.5
  249.7 1.6 fusion.46
  251.3 1.0 constant_dynamic-slice_fusion.5
  252.5 1.6 fusion.46
  254.0 1.0 constant_dynamic-slice_fusion.5
  255.2 1.6 fusion.46
  256.9 1.1 convolution_convert_fusion
  258.0 1.9 collective-permute-start
  259.9 4.3 %collective-permute-start.1 = (bf16[256,256]{1,0:T(8,128)(2,1)S(1)}, bf16[256,256]{1,0:T(8,128)(2,1)S(1)}, u32[]{:S(2)}, u32[]{:S(2)}) collective-permute-start(bf16[256,256]{1,0:T(8,128)(2,1)S(1)} %get-tuple-element.167), channel_id=1, source_target_pairs={{1,0},{2,1},{3,2},{4,3},{5,4},{6,5},{7,6},{8,7},{9,8},{10,9},{11,1... | collective-permute-start | bytes 393224 | tf_op jit(solution)/shard_map/ppermute | solution.py:28
  264.8 1.4 collective-permute-done.1
  266.2 1.1 convolution_add_fusion
  (51 shorter events, 5.4 us)
Async XLA Ops:
  6.5 1.2 copy-start
  6.5 59.2 %all-gather.9.cloned.1.call-start = ((), (), s32[]{:S(2)}) async-start(), calls=%async_computation | async-start | bytes 4456448 | tf_op jit(solution)/shard_map/all_gather | solution.py:13
  10.6 105.9 %all-gather.11.cloned.1.call-start = ((), (), s32[]{:S(2)}) async-start(), calls=%async_computation.1 | async-start | bytes 4456448 | tf_op jit(solution)/shard_map/all_gather | solution.py:13
  13.5 154.1 %all-gather.13.cloned.1.call-start = ((), (), s32[]{:S(2)}) async-start(), calls=%async_computation.2 | async-start | bytes 4456448 | tf_op jit(solution)/shard_map/all_gather | solution.py:13
  14.3 204.3 %all-gather.15.cloned.1.call-start = ((), (), s32[]{:S(2)}) async-start(), calls=%async_computation.3 | async-start | bytes 4456448 | tf_op jit(solution)/shard_map/all_gather | solution.py:13
  116.5 5.1 %copy-start.1 = (s32[512]{0:T(512)S(1)}, s32[512]{0:T(512)}, u32[]{:S(2)}) copy-start(s32[512]{0:T(512)} %param.13) | copy-start | bytes 6148
  258.0 6.6 %collective-permute-start = (bf16[256,256]{1,0:T(8,128)(2,1)S(1)}, bf16[256,256]{1,0:T(8,128)(2,1)S(1)}, u32[]{:S(2)}, u32[]{:S(2)}) collective-permute-start(bf16[256,256]{1,0:T(8,128)(2,1)S(1)} %get-tuple-element.168), channel_id=1, source_target_pairs={{0,1},{1,2},{2,3},{3,4},{4,5},{5,6},{6,7},{7,8},{8,9},{9,10},{10,1... | collective-permute-start | bytes 393224 | tf_op jit(solution)/shard_map/ppermute | solution.py:28
  259.9 6.3 %collective-permute-start.1 = (bf16[256,256]{1,0:T(8,128)(2,1)S(1)}, bf16[256,256]{1,0:T(8,128)(2,1)S(1)}, u32[]{:S(2)}, u32[]{:S(2)}) collective-permute-start(bf16[256,256]{1,0:T(8,128)(2,1)S(1)} %get-tuple-element.167), channel_id=1, source_target_pairs={{1,0},{2,1},{3,2},{4,3},{5,4},{6,5},{7,6},{8,7},{9,8},{10,9},{11,1... | collective-permute-start | bytes 393224 | tf_op jit(solution)/shard_map/ppermute | solution.py:28
Sparse Core Ops, SparseCore 0:
  10.8 54.9 all-gather.8
  67.9 48.5 all-gather.10
  118.7 48.8 all-gather.12
  169.6 48.8 all-gather.14
where the time goes:
time: 275 us; the launch traced here: 274 us
  waiting for transfers between devices  194 us (71%)
  matrix products  32.5 us (12%)
  local copies, waits for them, and re-layouts  24.5 us (9%)
  between operations  13.3 us (5%)
  starting transfers between devices  6.32 us (2%)
    all_gather x4, waiting for transfers between devices, entering(): gathered = jax.tree.map(lambda a: lax.all_gather(a, axis), part)  192 us
    dot_general x15, matrix products, compose(): jnp.dot(earlier[1], later[0], precision=precise) + later[1]  23.3 us
    dynamic_slice x30, local copies, waits for them, and re-layouts, one(): lax.dynamic_index_in_dim(a, source, 0, False)  16.5 us
    ppermute x2, starting transfers between devices, from_behind(): return lax.ppermute(block, axis, route)  6.2 us
    while x2, local copies, waits for them, and re-layouts, entering(): return lax.fori_loop(0, ahead, one, state)  5.76 us
  transfers between devices with their start and end apart: 6, of which 5 were waited for; matrix products, arithmetic and copies ran while one was open for 6% of the time, Pallas kernels for 0%

commit v1 on v0

v1 whole, which is shorter than its diff:
```python
import functools

import jax
import jax.numpy as jnp
from jax import lax
from jax.experimental import pallas as pl
from jax.experimental.pallas import tpu as pltpu
from jax.sharding import PartitionSpec as P

F32 = jnp.float32
BF16 = jnp.bfloat16
NN = (((1,), (0,)), ((), ()))
NT = (((1,), (1,)), ((), ()))


def halves(x):
    high = x.astype(BF16)
    return high, (x - high.astype(F32)).astype(BF16)


def product(a, b, dims):
    return lax.dot_general(a, b, dims, preferred_element_type=F32)


def dot3(a, b, dims):
    return product(a[0], b[0], dims) + (product(a[0], b[1], dims) + product(a[1], b[0], dims))


def stacked(b):
    return jnp.concatenate([b[0], b[0], b[1]], axis=0)


def dot_stacked(x, weights):
    high, low = halves(x)
    return product(jnp.concatenate([high, low, high], axis=1), weights, NN)


def kernel(
    n, z_ref, inverse_ref, couple_ref, coef_ref, anchor_ref, out_ref,
    tail_in, tail_out, upper_in, upper_out, left_in, right_in, left_out, right_out,
    top_rows, forward_w, backward_w, inv_hi, inv_lo, proj_hi, proj_lo, masked,
    fs, fr, bs, br, es, er,
):
    me = lax.axis_index("genome")
    first, last = me == 0, me == n - 1
    right, left = lax.rem(me + 1, n), lax.rem(me + n - 1, n)
    chunks, rows, half = tail_in.shape
    typed = inverse_ref.shape[0]
    top = typed - half
    traits = chunks * rows

    barrier = pltpu.get_barrier_semaphore()
    for other in (left, right):
        pl.semaphore_signal(barrier, inc=1, device_id={"genome": other},
                            device_id_type=pl.DeviceIdType.MESH)

    def remote(src, dst, send, recv, other):
        return pltpu.make_async_remote_copy(
            src_ref=src, dst_ref=dst, send_sem=send, recv_sem=recv,
            device_id={"genome": other}, device_id_type=pl.DeviceIdType.MESH)

    def forward_copy(c):
        return remote(tail_out.at[c], tail_in.at[c], fs.at[c], fr.at[c], right)

    def backward_copy(c):
        return remote(upper_out.at[c], upper_in.at[c], bs.at[c], br.at[c], left)

    def to_right():
        return remote(left_out, left_in, es.at[0], er.at[0], right)

    def to_left():
        return remote(right_out, right_in, es.at[1], er.at[1], left)

    hi, lo = halves(inverse_ref[...])
    inv_hi[...] = hi
    inv_lo[...] = lo
    z_halves = halves(z_ref[...])
    solved_tail = dot3(z_halves, (inv_hi[pl.ds(top, half), :], inv_lo[pl.ds(top, half), :]), NT)
    tail_out[...] = solved_tail.reshape(chunks, rows, half)
    pl.semaphore_wait(barrier, 2)

    @pl.when(first)
    def _():
        def go(c, _):
            forward_copy(c).start()
            return 0
        lax.fori_loop(0, chunks, go, 0)
        tail_in[...] = jnp.zeros_like(tail_in)
        left_in[...] = jnp.zeros_like(left_in)

    @pl.when(last)
    def _():
        upper_in[...] = jnp.zeros_like(upper_in)
        right_in[...] = jnp.zeros_like(right_in)

    projected = dot3((inv_hi[...], inv_lo[...]), halves(couple_ref[...]), NN)
    hi, lo = halves(projected)
    proj_hi[...] = hi
    proj_lo[...] = lo
    chain = -projected[top:, :]
    forward_w[...] = stacked(halves(chain.T))
    backward_w[...] = stacked(halves(chain))
    solved_top = dot3(z_halves, (inv_hi[pl.ds(0, top), :], inv_lo[pl.ds(0, top), :]), NT)
    top_rows[...] = solved_top.reshape(chunks, rows, top)

    def make_mask():
        spread = 128
        units = anchor_ref.shape[1]
        nearest = jnp.broadcast_to(anchor_ref[...], (spread, units)).T
        start = me * typed - half
        lanes = lax.broadcasted_iota(jnp.int32, (units, spread), 1)
        for j in range(0, typed + 2 * half, spread):
            within = jnp.abs(lanes + (start + j) - nearest) <= half
            coef = coef_ref[:, j:j + spread].astype(F32)
            masked[:, j:j + spread] = jnp.where(within, coef, 0.0).astype(BF16)

    @pl.when(me >= n // 2)
    def _():
        make_mask()

    def source(tail, above, below):
        above = above - dot3(halves(tail), (proj_hi[pl.ds(0, top), :], proj_lo[pl.ds(0, top), :]), NT)
        all_rows = jnp.concatenate([above, below], axis=1)
        return above, dot3(halves(all_rows), (proj_hi[...], proj_lo[...]), NN)

    @pl.when(jnp.logical_not(first))
    def _():
        def step(c, _):
            forward_copy(c).wait_recv()
            tail_out[c] = tail_out[c] + dot_stacked(tail_in[c], forward_w[...])

            @pl.when(jnp.logical_not(last))
            def _():
                forward_copy(c).start()

            @pl.when(last)
            def _():
                above, add = source(tail_in[c], top_rows[c], tail_out[c])
                top_rows[c] = above
                upper_out[c] = add
                backward_copy(c).start()
            return 0
        lax.fori_loop(0, chunks, step, 0)

    @pl.when(jnp.logical_not(last))
    def _():
        above, add = source(tail_in[...].reshape(traits, half), top_rows[...].reshape(traits, top),
                            tail_out[...].reshape(traits, half))
        top_rows[...] = above.reshape(chunks, rows, top)
        upper_out[...] = add.reshape(chunks, rows, half)

    @pl.when(me < n // 2)
    def _():
        make_mask()

    @pl.when(jnp.logical_not(last))
    def _():
        def step(c, _):
            backward_copy(c).wait_recv()

            @pl.when(jnp.logical_not(first))
            def _():
                upper_out[c] = upper_out[c] + dot_stacked(upper_in[c], backward_w[...])
                backward_copy(c).start()
            return 0
        lax.fori_loop(0, chunks, step, 0)

    below = (tail_out[...] - upper_in[...]).reshape(traits, half)
    rows_now = jnp.concatenate([top_rows[...].reshape(traits, top), below], axis=1)
    weights = dot3(halves(rows_now), (inv_hi[...], inv_lo[...]), NN).astype(BF16)
    left_out[...] = weights[:, top:]
    right_out[...] = weights[:, :half]

    @pl.when(jnp.logical_not(last))
    def _():
        to_right().start()

    @pl.when(jnp.logical_not(first))
    def _():
        to_left().start()

    out_ref[...] = product(weights, masked[:, half:half + typed], NT)

    @pl.when(jnp.logical_not(last))
    def _():
        to_left().wait_recv()

    out_ref[...] += product(right_in[...], masked[:, half + typed:], NT)

    @pl.when(jnp.logical_not(first))
    def _():
        to_right().wait_recv()

    out_ref[...] += product(left_in[...], masked[:, :half], NT)

    @pl.when(jnp.logical_not(last))
    def _():
        def done(c, _):
            forward_copy(c).wait_send()
            return 0
        lax.fori_loop(0, chunks, done, 0)
        to_right().wait_send()

    @pl.when(jnp.logical_not(first))
    def _():
        def done(c, _):
            backward_copy(c).wait_send()
            return 0
        lax.fori_loop(0, chunks, done, 0)
        to_left().wait_send()


def per_device(n, z_typed, diag_inverse, coupling, impute_coef, anchor):
    traits, typed = z_typed.shape
    half = coupling.shape[2]
    units, span = impute_coef.shape
    top = typed - half
    chunks = next(k for k in (8, 4, 2, 1) if traits % (16 * k) == 0 or k == 1)
    rows = traits // chunks
    state = pltpu.VMEM((chunks, rows, half), F32)
    edge = pltpu.VMEM((traits, half), BF16)
    sems = pltpu.SemaphoreType.DMA((chunks,))
    return pl.pallas_call(
        functools.partial(kernel, n),
        out_shape=jax.ShapeDtypeStruct((traits, units), F32),
        in_specs=[pl.BlockSpec(memory_space=pltpu.VMEM)] * 5,
        out_specs=pl.BlockSpec(memory_space=pltpu.VMEM),
        scratch_shapes=[
            state, state, state, state, edge, edge, edge, edge,
            pltpu.VMEM((chunks, rows, top), F32),
            pltpu.VMEM((3 * half, half), BF16), pltpu.VMEM((3 * half, half), BF16),
            pltpu.VMEM((typed, typed), BF16), pltpu.VMEM((typed, typed), BF16),
            pltpu.VMEM((typed, half), BF16), pltpu.VMEM((typed, half), BF16),
            pltpu.VMEM((units, span), BF16),
            sems, sems, sems, sems,
            pltpu.SemaphoreType.DMA((2,)), pltpu.SemaphoreType.DMA((2,)),
        ],
        compiler_params=pltpu.CompilerParams(
            collective_id=0, has_side_effects=True, vmem_limit_bytes=48 * 1024 * 1024),
    )(z_typed, diag_inverse[0], coupling[0], impute_coef, anchor.reshape(1, units))


def solution(mesh):
    shared = ("seg", "genome")
    in_specs = (P(None, shared), P(shared, None, None), P(shared, None, None),
                P(shared, None), P(shared))
    return jax.shard_map(
        functools.partial(per_device, mesh.shape["genome"]), mesh=mesh, in_specs=in_specs,
        out_specs=P(None, shared), check_vma=False)
```

time: 275 us -> 78.3 us (0.28)
  waiting for transfers between devices: 194 us -> 0 us
  Pallas kernels: 0 us -> 72 us
  matrix products: 32.5 us -> 0 us
  local copies, waits for them, and re-layouts: 24.5 us -> 6.01 us
  between operations: 13.3 us -> 0.01 us
  starting transfers between devices: 6.32 us -> 0 us
    all_gather x4 -> x0, waiting for transfers between devices: 192 us -> none  [entering(): gathered = jax.tree.map(lambda a: lax.all_gather(a, axis), part)]
    pallas_call x0 -> x1, Pallas kernels: none -> 72 us  [per_device(): pl.pallas_call(functools.partial(kernel, n), out_shape=jax.ShapeDtypeStru...]
    dot_general x23 -> x0, matrix products: 32.5 us -> none  [the longest x15 23.3 us: compose(): jnp.dot(earlier[1], later[0], precision=precise) + later[1]]
    dynamic_slice x30 -> x0, local copies, waits for them, and re-layouts: 16.5 us -> none  [one(): lax.dynamic_index_in_dim(a, source, 0, False)]
    ppermute x2 -> x0, starting transfers between devices: 6.2 us -> none  [from_behind(): return lax.ppermute(block, axis, route)]
    while x17 -> x0, local copies, waits for them, and re-layouts: 6.04 us -> none  [the longest x2 5.76 us: entering(): return lax.fori_loop(0, ahead, one, state)]
    unnamed x4 -> x11, local copies, waits for them, and re-layouts: 1.23 us -> 6.01 us
  transfers between devices with their start and end apart: 6 -> 0, of which waited for: 5 -> 0; matrix products, arithmetic and copies ran while one was open for 6% -> 0% of each run, Pallas kernels for 0% -> 0%
where the time goes in v1:
time: 78.3 us; the launch traced here: 78 us
  Pallas kernels  72 us (92%)
  local copies, waits for them, and re-layouts  6.01 us (8%)
    pallas_call x1, Pallas kernels, per_device(): pl.pallas_call(functools.partial(kernel, n), out_shape=jax.ShapeDtypeStru...  72 us
    unnamed x11, local copies, waits for them, and re-layouts  6.01 us

profile of v1, /device:TPU:1, one launch (start us, length us, event | category | flops | bytes accessed | tf_op | source)
XLA Modules:
  0.0 78.0 jit_solution(1884316757481991012)
XLA Ops:
  0.0 0.0 copy-start.4
  0.0 0.7 copy-done.4
  0.7 0.0 copy-start
  0.7 1.2 %copy-done = f32[1,512,512]{2,1,0:T(8,128)S(1)} copy-done((f32[1,512,512]{2,1,0:T(8,128)S(1)}, f32[1,512,512]{2,1,0:T(8,128)}, u32[]{:S(2)}) %copy-start) | copy-done | bytes 1048600
  1.9 0.0 copy-start.1
  1.9 1.2 %copy-done.1 = bf16[512,1024]{1,0:T(8,128)(2,1)S(1)} copy-done((bf16[512,1024]{1,0:T(8,128)(2,1)S(1)}, bf16[512,1024]{1,0:T(8,128)(2,1)}, u32[]{:S(2)}) %copy-start.1) | copy-done | bytes 1048600
  3.1 0.0 copy-start.2
  3.1 1.0 %copy-done.2 = f32[256,512]{1,0:T(8,128)S(1)} copy-done((f32[256,512]{1,0:T(8,128)S(1)}, f32[256,512]{1,0:T(8,128)}, u32[]{:S(2)}) %copy-start.2) | copy-done | bytes 524312
  4.2 0.0 copy-start.3
  4.2 1.0 %copy-done.3 = f32[1,512,256]{2,1,0:T(8,128)S(1)} copy-done((f32[1,512,256]{2,1,0:T(8,128)S(1)}, f32[1,512,256]{2,1,0:T(8,128)}, u32[]{:S(2)}) %copy-start.3) | copy-done | bytes 524312
  5.2 72.0 %shard_map.55 = f32[256,512]{1,0:T(8,128)S(1)} custom-call(f32[256,512]{1,0:T(8,128)S(1)} %copy-done.2, f32[512,512]{1,0:T(8,128)S(1)} %bitcast.3, f32[512,256]{1,0:T(8,128)S(1)} %bitcast.4, bf16[512,1024]{1,0:T(8,128)(2,1)S(1)} %copy-done.1, s32[1,512]{1,0:T(1,128)S(1)} %bitcast.5), custom_call_target="tpu_custom_call" | custom-call | tf_op jit(solution)/shard_map/pallas_call | solution.py:223
  77.2 0.8 %copy.7 = f32[256,512]{1,0:T(8,128)} copy(f32[256,512]{1,0:T(8,128)S(1)} %shard_map.55) | data formatting | bytes 1048576
Async XLA Ops:
  0.0 0.7 copy-start.4
  0.7 1.2 %copy-start = (f32[1,512,512]{2,1,0:T(8,128)S(1)}, f32[1,512,512]{2,1,0:T(8,128)}, u32[]{:S(2)}) copy-start(f32[1,512,512]{2,1,0:T(8,128)} %param.6) | copy-start | bytes 3145732
  1.9 1.2 %copy-start.1 = (bf16[512,1024]{1,0:T(8,128)(2,1)S(1)}, bf16[512,1024]{1,0:T(8,128)(2,1)}, u32[]{:S(2)}) copy-start(bf16[512,1024]{1,0:T(8,128)(2,1)} %coef_ref.1) | copy-start | bytes 3145732
  3.1 1.0 %copy-start.2 = (f32[256,512]{1,0:T(8,128)S(1)}, f32[256,512]{1,0:T(8,128)}, u32[]{:S(2)}) copy-start(f32[256,512]{1,0:T(8,128)} %z_ref.1) | copy-start | bytes 1572868
  4.2 1.0 %copy-start.3 = (f32[1,512,256]{2,1,0:T(8,128)S(1)}, f32[1,512,256]{2,1,0:T(8,128)}, u32[]{:S(2)}) copy-start(f32[1,512,256]{2,1,0:T(8,128)} %param.7) | copy-start | bytes 1572868

commit v2 on v1

v2 whole, which is shorter than its diff:
```python
import functools

import jax
import jax.numpy as jnp
from jax import lax
from jax.experimental import pallas as pl
from jax.experimental.pallas import tpu as pltpu
from jax.sharding import PartitionSpec as P

F32 = jnp.float32
BF16 = jnp.bfloat16
NN = (((1,), (0,)), ((), ()))
NT = (((1,), (1,)), ((), ()))


def halves(x):
    high = x.astype(BF16)
    return high, (x - high.astype(F32)).astype(BF16)


def product(a, b, dims):
    return lax.dot_general(a, b, dims, preferred_element_type=F32)


def dot3(a, b, dims):
    return product(a[0], b[0], dims) + (product(a[0], b[1], dims) + product(a[1], b[0], dims))


def stacked(b):
    return jnp.concatenate([b[0], b[0], b[1]], axis=0)


def dot_stacked(x, weights):
    high, low = halves(x)
    return product(jnp.concatenate([high, low, high], axis=1), weights, NN)


def kernel(
    n, group, z_ref, inverse_ref, couple_ref, coef_ref, anchor_ref, out_ref,
    tail_in, tail_out, upper_in, upper_out, enter_f, enter_b, solved_tail,
    map_f_in, map_f_out, map_b_in, map_b_out, left_in, right_in, left_out, right_out,
    top_rows, forward_w, backward_w, inv_hi, inv_lo, proj_hi, proj_lo, masked,
    sent, got, es, er,
):
    me = lax.axis_index("genome")
    count = n // group
    g, q = me // group, lax.rem(me, group)
    first, last = me == 0, me == n - 1
    head, tail = q == 0, q == group - 1
    start_group, end_group = g == 0, g == count - 1
    right, left = lax.rem(me + 1, n), lax.rem(me + n - 1, n)
    far_right, far_left = lax.rem(me + group, n), lax.rem(me + n - group, n)
    chunks, rows, half = tail_in.shape
    typed = inverse_ref.shape[0]
    top = typed - half
    traits = chunks * rows
    no = jnp.logical_not

    def both(*conditions):
        return functools.reduce(jnp.logical_and, conditions)

    barrier = pltpu.get_barrier_semaphore()
    for other in (left, right, far_left, far_right):
        pl.semaphore_signal(barrier, inc=1, device_id={"genome": other},
                            device_id_type=pl.DeviceIdType.MESH)

    def remote(src, dst, send, recv, other):
        return pltpu.make_async_remote_copy(
            src_ref=src, dst_ref=dst, send_sem=send, recv_sem=recv,
            device_id={"genome": other}, device_id_type=pl.DeviceIdType.MESH)

    def channel(index, src, dst, landing, other):
        return lambda c: remote(src.at[c], dst.at[c], sent.at[index, c], got.at[landing, c], other)

    map_f = channel(0, map_f_out, map_f_in, 0, right)
    local_f = channel(1, tail_out, tail_in, 1, right)
    group_f = channel(2, tail_out, enter_f, 2, far_right)
    pass_f = channel(3, enter_f, enter_f, 2, left)
    map_b = channel(4, map_b_out, map_b_in, 3, left)
    local_b = channel(5, upper_out, upper_in, 4, left)
    group_b = channel(6, upper_out, enter_b, 5, far_left)
    pass_b = channel(7, enter_b, enter_b, 5, right)

    def to_right():
        return remote(left_out, left_in, es.at[0], er.at[0], right)

    def to_left():
        return remote(right_out, right_in, es.at[1], er.at[1], left)

    def each(condition, step):
        @pl.when(condition)
        def _():
            def go(c, _):
                step(c)
                return 0
            lax.fori_loop(0, chunks, go, 0)

    def clear(condition, ref):
        @pl.when(condition)
        def _():
            ref[...] = jnp.zeros_like(ref)

    def unit(condition, ref):
        @pl.when(condition)
        def _():
            row = lax.broadcasted_iota(jnp.int32, (half, half), 0)
            col = lax.broadcasted_iota(jnp.int32, (half, half), 1)
            ref[...] = (row == col).astype(F32).reshape(ref.shape)

    hi, lo = halves(inverse_ref[...])
    inv_hi[...] = hi
    inv_lo[...] = lo
    z_halves = halves(z_ref[...])
    solved = dot3(z_halves, (inv_hi[pl.ds(top, half), :], inv_lo[pl.ds(top, half), :]), NT)
    tail_out[...] = solved.reshape(chunks, rows, half)
    solved_tail[...] = solved.reshape(chunks, rows, half)
    pl.semaphore_wait(barrier, 4)

    each(both(head, start_group, no(tail)), lambda c: local_f(c).start())

    projected = dot3((inv_hi[...], inv_lo[...]), halves(couple_ref[...]), NN)
    hi, lo = halves(projected)
    proj_hi[...] = hi
    proj_lo[...] = lo
    chain = -projected[top:, :]
    chain_t = chain.T
    map_f_out[...] = chain_t.reshape(map_f_out.shape)
    map_b_out[...] = chain.reshape(map_b_out.shape)
    forward_w[...] = stacked(halves(chain_t))
    backward_w[...] = stacked(halves(chain))

    def start_head(c):
        map_f(c).start()
    each(both(head, no(start_group), no(tail)), start_head)
    each(both(head, no(start_group), no(tail)), lambda c: local_f(c).start())
    each(both(tail, no(end_group), no(head)), lambda c: map_b(c).start())

    clear(head, tail_in)
    clear(tail, upper_in)
    clear(start_group, enter_f)
    clear(end_group, enter_b)
    clear(first, left_in)
    clear(last, right_in)
    unit(jnp.logical_or(head, start_group), map_f_in)
    unit(jnp.logical_or(tail, end_group), map_b_in)

    def step(c):
        map_f(c).wait_recv()
        map_f_out[c] = dot_stacked(map_f_in[c], forward_w[...])

        @pl.when(no(tail))
        def _():
            map_f(c).start()
    each(both(no(start_group), no(head)), step)

    def step(c):
        local_f(c).wait_recv()
        tail_out[c] = tail_out[c] + dot_stacked(tail_in[c], forward_w[...])

        @pl.when(no(tail))
        def _():
            local_f(c).start()

        @pl.when(both(tail, start_group, no(end_group)))
        def _():
            group_f(c).start()
    each(no(head), step)
    if group == 1:
        each(both(start_group, no(end_group)), lambda c: group_f(c).start())

    solved_top = dot3(z_halves, (inv_hi[pl.ds(0, top), :], inv_lo[pl.ds(0, top), :]), NT)
    top_rows[...] = solved_top.reshape(chunks, rows, top)

    def step(c):
        map_b(c).wait_recv()
        map_b_out[c] = dot_stacked(map_b_in[c], backward_w[...])

        @pl.when(no(head))
        def _():
            map_b(c).start()
    each(both(no(end_group), no(tail)), step)

    def make_mask():
        spread = 128
        units = anchor_ref.shape[1]
        nearest = jnp.broadcast_to(anchor_ref[...], (spread, units)).T
        start = me * typed - half
        lanes = lax.broadcasted_iota(jnp.int32, (units, spread), 1)
        for j in range(0, typed + 2 * half, spread):
            within = jnp.abs(lanes + (start + j) - nearest) <= half
            coef = coef_ref[:, j:j + spread].astype(F32)
            masked[:, j:j + spread] = jnp.where(within, coef, 0.0).astype(BF16)

    @pl.when(g >= count // 2)
    def _():
        make_mask()

    @pl.when(both(no(start_group), tail))
    def _():
        whole = stacked(halves(map_f_out[...].reshape(half, half)))

        def go(c, _):
            group_f(c).wait_recv()

            if group > 1:
                pass_f(c).start()
            tail_out[c] = tail_out[c] + dot_stacked(enter_f[c], whole)

            @pl.when(no(end_group))
            def _():
                group_f(c).start()
            return 0
        lax.fori_loop(0, chunks, go, 0)

    def step(c):
        pass_f(c).wait_recv()

        @pl.when(no(head))
        def _():
            pass_f(c).start()
    each(both(no(start_group), no(tail)), step)

    before = tail_in[...].reshape(traits, half) + dot_stacked(
        enter_f[...].reshape(traits, half), stacked(halves(map_f_in[...].reshape(half, half))))
    below = solved_tail[...].reshape(traits, half) + dot_stacked(before, forward_w[...])
    above = top_rows[...].reshape(traits, top) - dot3(
        halves(before), (proj_hi[pl.ds(0, top), :], proj_lo[pl.ds(0, top), :]), NT)
    add = dot3(halves(jnp.concatenate([above, below], axis=1)), (proj_hi[...], proj_lo[...]), NN)
    upper_out[...] = add.reshape(chunks, rows, half)
    each(both(tail, no(head)), lambda c: local_b(c).start())
    solved_tail[...] = below.reshape(chunks, rows, half)
    top_rows[...] = above.reshape(chunks, rows, top)

    def step(c):
        local_b(c).wait_recv()
        upper_out[c] = upper_out[c] + dot_stacked(upper_in[c], backward_w[...])

        @pl.when(no(head))
        def _():
            local_b(c).start()

        @pl.when(both(head, end_group, no(start_group)))
        def _():
            group_b(c).start()
    each(no(tail), step)
    if group == 1:
        each(both(end_group, no(start_group)), lambda c: group_b(c).start())

    @pl.when(both(no(end_group), head))
    def _():
        whole = stacked(halves(map_b_out[...].reshape(half, half)))

        def go(c, _):
            group_b(c).wait_recv()

            if group > 1:
                pass_b(c).start()

            @pl.when(no(start_group))
            def _():
                upper_out[c] = upper_out[c] + dot_stacked(enter_b[c], whole)
                group_b(c).start()
            return 0
        lax.fori_loop(0, chunks, go, 0)

    @pl.when(g < count // 2)
    def _():
        make_mask()

    def step(c):
        pass_b(c).wait_recv()

        @pl.when(no(tail))
        def _():
            pass_b(c).start()
    each(both(no(end_group), no(head)), step)

    after = upper_in[...].reshape(traits, half) + dot_stacked(
        enter_b[...].reshape(traits, half), stacked(halves(map_b_in[...].reshape(half, half))))
    rows_now = jnp.concatenate(
        [top_rows[...].reshape(traits, top), solved_tail[...].reshape(traits, half) - after], axis=1)
    weights = dot3(halves(rows_now), (inv_hi[...], inv_lo[...]), NN).astype(BF16)
    left_out[...] = weights[:, top:]
    right_out[...] = weights[:, :half]

    @pl.when(no(last))
    def _():
        to_right().start()

    @pl.when(no(first))
    def _():
        to_left().start()

    out_ref[...] = product(weights, masked[:, half:half + typed], NT)

    @pl.when(no(last))
    def _():
        to_left().wait_recv()

    out_ref[...] += product(right_in[...], masked[:, half + typed:], NT)

    @pl.when(no(first))
    def _():
        to_right().wait_recv()

    out_ref[...] += product(left_in[...], masked[:, :half], NT)

    each(both(no(start_group), no(tail)), lambda c: map_f(c).wait_send())
    each(no(tail), lambda c: local_f(c).wait_send())
    each(both(tail, no(end_group)), lambda c: group_f(c).wait_send())
    each(both(no(head), no(start_group)), lambda c: pass_f(c).wait_send())
    each(both(no(end_group), no(head)), lambda c: map_b(c).wait_send())
    each(no(head), lambda c: local_b(c).wait_send())
    each(both(head, no(start_group)), lambda c: group_b(c).wait_send())
    each(both(no(tail), no(end_group)), lambda c: pass_b(c).wait_send())

    @pl.when(no(last))
    def _():
        to_right().wait_send()

    @pl.when(no(first))
    def _():
        to_left().wait_send()


def per_device(n, z_typed, diag_inverse, coupling, impute_coef, anchor):
    traits, typed = z_typed.shape
    half = coupling.shape[2]
    units, span = impute_coef.shape
    top = typed - half
    chunks = next(k for k in (8, 4, 2, 1) if traits % (16 * k) == half % (8 * k) == 0 or k == 1)
    rows = traits // chunks
    group = 1
    while n % (2 * group) == 0 and 4 * group * group <= n:
        group *= 2
    state = pltpu.VMEM((chunks, rows, half), F32)
    edge = pltpu.VMEM((traits, half), BF16)
    chain_map = pltpu.VMEM((chunks, half // chunks, half), F32)
    return pl.pallas_call(
        functools.partial(kernel, n, group),
        out_shape=jax.ShapeDtypeStruct((traits, units), F32),
        in_specs=[pl.BlockSpec(memory_space=pltpu.VMEM)] * 5,
        out_specs=pl.BlockSpec(memory_space=pltpu.VMEM),
        scratch_shapes=[
            state, state, state, state, state, state, state,
            chain_map, chain_map, chain_map, chain_map, edge, edge, edge, edge,
            pltpu.VMEM((chunks, rows, top), F32),
            pltpu.VMEM((3 * half, half), BF16), pltpu.VMEM((3 * half, half), BF16),
            pltpu.VMEM((typed, typed), BF16), pltpu.VMEM((typed, typed), BF16),
            pltpu.VMEM((typed, half), BF16), pltpu.VMEM((typed, half), BF16),
            pltpu.VMEM((units, span), BF16),
            pltpu.SemaphoreType.DMA((8, chunks)), pltpu.SemaphoreType.DMA((6, chunks)),
            pltpu.SemaphoreType.DMA((2,)), pltpu.SemaphoreType.DMA((2,)),
        ],
        compiler_params=pltpu.CompilerParams(
            collective_id=0, has_side_effects=True, vmem_limit_bytes=48 * 1024 * 1024),
    )(z_typed, diag_inverse[0], coupling[0], impute_coef, anchor.reshape(1, units))


def solution(mesh):
    shared = ("seg", "genome")
    in_specs = (P(None, shared), P(shared, None, None), P(shared, None, None),
                P(shared, None), P(shared))
    return jax.shard_map(
        functools.partial(per_device, mesh.shape["genome"]), mesh=mesh, in_specs=in_specs,
        out_specs=P(None, shared), check_vma=False)
```

time: 78.3 us -> 57.3 us (0.73)
  Pallas kernels: 72 us -> 51 us
    pallas_call x1, Pallas kernels: 72 us -> 51 us  [per_device(): pl.pallas_call(functools.partial(kernel, n, group), out_shape=jax.ShapeDt...]
where the time goes in v2:
time: 57.3 us; the launch traced here: 57 us
  Pallas kernels  51 us (89%)
  local copies, waits for them, and re-layouts  6.01 us (10%)
    pallas_call x1, Pallas kernels, per_device(): pl.pallas_call(functools.partial(kernel, n, group), out_shape=jax.ShapeDt...  51 us
    unnamed x11, local copies, waits for them, and re-layouts  6.01 us

profile of v2, /device:TPU:1, one launch (start us, length us, event | category | flops | bytes accessed | tf_op | source)
XLA Modules:
  0.0 57.0 jit_solution(462709314666260245)
XLA Ops:
  0.0 0.0 copy-start.4
  0.0 0.7 %copy-done.4 = s32[512]{0:T(512)S(1)} copy-done((s32[512]{0:T(512)S(1)}, s32[512]{0:T(512)}, u32[]{:S(2)}) %copy-start.4) | copy-done | bytes 2072
  0.7 0.0 copy-start
  0.7 1.2 %copy-done = f32[1,512,512]{2,1,0:T(8,128)S(1)} copy-done((f32[1,512,512]{2,1,0:T(8,128)S(1)}, f32[1,512,512]{2,1,0:T(8,128)}, u32[]{:S(2)}) %copy-start) | copy-done | bytes 1048600
  1.9 0.0 copy-start.1
  1.9 1.2 %copy-done.1 = bf16[512,1024]{1,0:T(8,128)(2,1)S(1)} copy-done((bf16[512,1024]{1,0:T(8,128)(2,1)S(1)}, bf16[512,1024]{1,0:T(8,128)(2,1)}, u32[]{:S(2)}) %copy-start.1) | copy-done | bytes 1048600
  3.1 0.0 copy-start.2
  3.1 1.0 %copy-done.2 = f32[256,512]{1,0:T(8,128)S(1)} copy-done((f32[256,512]{1,0:T(8,128)S(1)}, f32[256,512]{1,0:T(8,128)}, u32[]{:S(2)}) %copy-start.2) | copy-done | bytes 524312
  4.2 0.0 copy-start.3
  4.2 1.0 %copy-done.3 = f32[1,512,256]{2,1,0:T(8,128)S(1)} copy-done((f32[1,512,256]{2,1,0:T(8,128)S(1)}, f32[1,512,256]{2,1,0:T(8,128)}, u32[]{:S(2)}) %copy-start.3) | copy-done | bytes 524312
  5.2 51.0 %shard_map.55 = f32[256,512]{1,0:T(8,128)S(1)} custom-call(f32[256,512]{1,0:T(8,128)S(1)} %copy-done.2, f32[512,512]{1,0:T(8,128)S(1)} %bitcast.3, f32[512,256]{1,0:T(8,128)S(1)} %bitcast.4, bf16[512,1024]{1,0:T(8,128)(2,1)S(1)} %copy-done.1, s32[1,512]{1,0:T(1,128)S(1)} %bitcast.5), custom_call_target="tpu_custom_call" | custom-call | tf_op jit(solution)/shard_map/pallas_call | solution.py:339
  56.2 0.8 %copy.7 = f32[256,512]{1,0:T(8,128)} copy(f32[256,512]{1,0:T(8,128)S(1)} %shard_map.55) | data formatting | bytes 1048576
Async XLA Ops:
  0.0 0.7 %copy-start.4 = (s32[512]{0:T(512)S(1)}, s32[512]{0:T(512)}, u32[]{:S(2)}) copy-start(s32[512]{0:T(512)} %param.9) | copy-start | bytes 6148
  0.7 1.2 %copy-start = (f32[1,512,512]{2,1,0:T(8,128)S(1)}, f32[1,512,512]{2,1,0:T(8,128)}, u32[]{:S(2)}) copy-start(f32[1,512,512]{2,1,0:T(8,128)} %param.6) | copy-start | bytes 3145732
  1.9 1.2 %copy-start.1 = (bf16[512,1024]{1,0:T(8,128)(2,1)S(1)}, bf16[512,1024]{1,0:T(8,128)(2,1)}, u32[]{:S(2)}) copy-start(bf16[512,1024]{1,0:T(8,128)(2,1)} %coef_ref.1) | copy-start | bytes 3145732
  3.1 1.0 %copy-start.2 = (f32[256,512]{1,0:T(8,128)S(1)}, f32[256,512]{1,0:T(8,128)}, u32[]{:S(2)}) copy-start(f32[256,512]{1,0:T(8,128)} %z_ref.1) | copy-start | bytes 1572868
  4.2 1.0 %copy-start.3 = (f32[1,512,256]{2,1,0:T(8,128)S(1)}, f32[1,512,256]{2,1,0:T(8,128)}, u32[]{:S(2)}) copy-start(f32[1,512,256]{2,1,0:T(8,128)} %param.7) | copy-start | bytes 1572868

commit v3 on v2

--- a/solution.py
+++ b/solution.py
@@ -36,10 +36,11 @@
 
 
 def kernel(
-    n, group, z_ref, inverse_ref, couple_ref, coef_ref, anchor_ref, out_ref,
-    tail_in, tail_out, upper_in, upper_out, enter_f, enter_b, solved_tail,
+    n, group, z_hbm, inverse_hbm, couple_hbm, coef_hbm, anchor_hbm, out_ref,
+    z_ref, inverse_ref, couple_ref, coef_ref, anchor_ref, fetched,
+    tail_in, tail_out, upper_in, upper_out, enter_f, enter_b, carry_f,
     map_f_in, map_f_out, map_b_in, map_b_out, left_in, right_in, left_out, right_out,
-    top_rows, forward_w, backward_w, inv_hi, inv_lo, proj_hi, proj_lo, masked,
+    top_rows, base, enter_rows_w, enter_add_w, enter_base_w, forward_w, backward_w, inv_hi, inv_lo, proj_hi, proj_lo, masked,
     sent, got, es, er,
 ):
     me = lax.axis_index("genome")
@@ -55,12 +56,21 @@
     top = typed - half
     traits = chunks * rows
     no = jnp.logical_not
+    even = lax.rem(q, 2) == 0
+    fetch = [
+        pltpu.make_async_copy(src, dst, fetched.at[i])
+        for i, (src, dst) in enumerate((
+            (inverse_hbm, inverse_ref), (z_hbm, z_ref), (couple_hbm, couple_ref),
+            (anchor_hbm, anchor_ref), (coef_hbm, coef_ref)))]
+    for copy in fetch:
+        copy.start()
 
     def both(*conditions):
         return functools.reduce(jnp.logical_and, conditions)
 
     barrier = pltpu.get_barrier_semaphore()
-    for other in (left, right, far_left, far_right):
+    right_two, left_two = lax.rem(me + 2, n), lax.rem(me + n - 2, n)
+    for other in (left, right, left_two, right_two, far_left, far_right):
         pl.semaphore_signal(barrier, inc=1, device_id={"genome": other},
                             device_id_type=pl.DeviceIdType.MESH)
 
@@ -74,12 +84,32 @@
 
     map_f = channel(0, map_f_out, map_f_in, 0, right)
     local_f = channel(1, tail_out, tail_in, 1, right)
-    group_f = channel(2, tail_out, enter_f, 2, far_right)
+    group_f = channel(2, carry_f, enter_f, 2, far_right)
     pass_f = channel(3, enter_f, enter_f, 2, left)
     map_b = channel(4, map_b_out, map_b_in, 3, left)
     local_b = channel(5, upper_out, upper_in, 4, left)
     group_b = channel(6, upper_out, enter_b, 5, far_left)
     pass_b = channel(7, enter_b, enter_b, 5, right)
+    pass_f_two = channel(8, enter_f, enter_f, 2, left_two)
+    pass_b_two = channel(9, enter_b, enter_b, 5, right_two)
+
+    def pass_on_f(c):
+        @pl.when(no(even))
+        def _():
+            pass_f(c).start()
+
+        @pl.when(both(no(even), q >= 2))
+        def _():
+            pass_f_two(c).start()
+
+    def pass_on_b(c):
+        @pl.when(both(even, q + 1 < group))
+        def _():
+            pass_b(c).start()
+
+        @pl.when(both(even, q + 2 < group))
+        def _():
+            pass_b_two(c).start()
 
     def to_right():
         return remote(left_out, left_in, es.at[0], er.at[0], right)
@@ -107,17 +137,19 @@
             col = lax.broadcasted_iota(jnp.int32, (half, half), 1)
             ref[...] = (row == col).astype(F32).reshape(ref.shape)
 
+    fetch[0].wait()
     hi, lo = halves(inverse_ref[...])
     inv_hi[...] = hi
     inv_lo[...] = lo
+    fetch[1].wait()
     z_halves = halves(z_ref[...])
     solved = dot3(z_halves, (inv_hi[pl.ds(top, half), :], inv_lo[pl.ds(top, half), :]), NT)
     tail_out[...] = solved.reshape(chunks, rows, half)
-    solved_tail[...] = solved.reshape(chunks, rows, half)
-    pl.semaphore_wait(barrier, 4)
+    pl.semaphore_wait(barrier, 6)
 
     each(both(head, start_group, no(tail)), lambda c: local_f(c).start())
 
+    fetch[2].wait()
     projected = dot3((inv_hi[...], inv_lo[...]), halves(couple_ref[...]), NN)
     hi, lo = halves(projected)
     proj_hi[...] = hi
@@ -163,10 +195,14 @@
 
         @pl.when(both(tail, start_group, no(end_group)))
         def _():
+            carry_f[c] = tail_out[c]
             group_f(c).start()
     each(no(head), step)
     if group == 1:
-        each(both(start_group, no(end_group)), lambda c: group_f(c).start())
+        def step(c):
+            carry_f[c] = tail_out[c]
+            group_f(c).start()
+        each(both(start_group, no(end_group)), step)
 
     solved_top = dot3(z_halves, (inv_hi[pl.ds(0, top), :], inv_lo[pl.ds(0, top), :]), NT)
     top_rows[...] = solved_top.reshape(chunks, rows, top)
@@ -179,6 +215,9 @@
         def _():
             map_b(c).start()
     each(both(no(end_group), no(tail)), step)
+
+    fetch[3].wait()
+    fetch[4].wait()
 
     def make_mask():
         spread = 128
@@ -195,41 +234,53 @@
     def _():
         make_mask()
 
-    @pl.when(both(no(start_group), tail))
+    def prepare():
+        proj = (proj_hi[...], proj_lo[...])
+        proj_top = (proj_hi[pl.ds(0, top), :], proj_lo[pl.ds(0, top), :])
+        above = top_rows[...].reshape(traits, top) - dot3(
+            halves(tail_in[...].reshape(traits, half)), proj_top, NT)
+        top_rows[...] = above.reshape(chunks, rows, top)
+        all_rows = jnp.concatenate([above, tail_out[...].reshape(traits, half)], axis=1)
+        upper_out[...] = dot3(halves(all_rows), proj, NN).reshape(chunks, rows, half)
+
+        @pl.when(no(start_group))
+        def _():
+            slope_top = -dot3(halves(map_f_in[...].reshape(half, half)), proj_top, NT)
+            slope = jnp.concatenate([slope_top, map_f_out[...].reshape(half, half)], axis=1)
+            slope_halves = halves(slope)
+            enter_rows_w[...] = stacked(slope_halves)
+            enter_add_w[...] = stacked(halves(dot3(slope_halves, proj, NN)))
+
+    relay = both(no(start_group), no(end_group), tail)
+
+    @pl.when(no(relay))
+    def _():
+        prepare()
+
+    @pl.when(relay)
     def _():
         whole = stacked(halves(map_f_out[...].reshape(half, half)))
 
         def go(c, _):
             group_f(c).wait_recv()
-
-            if group > 1:
-                pass_f(c).start()
-            tail_out[c] = tail_out[c] + dot_stacked(enter_f[c], whole)
-
-            @pl.when(no(end_group))
-            def _():
-                group_f(c).start()
+            pass_on_f(c)
+            carry_f[c] = tail_out[c] + dot_stacked(enter_f[c], whole)
+            group_f(c).start()
             return 0
         lax.fori_loop(0, chunks, go, 0)
-
-    def step(c):
-        pass_f(c).wait_recv()
-
-        @pl.when(no(head))
-        def _():
-            pass_f(c).start()
-    each(both(no(start_group), no(tail)), step)
-
-    before = tail_in[...].reshape(traits, half) + dot_stacked(
-        enter_f[...].reshape(traits, half), stacked(halves(map_f_in[...].reshape(half, half))))
-    below = solved_tail[...].reshape(traits, half) + dot_stacked(before, forward_w[...])
-    above = top_rows[...].reshape(traits, top) - dot3(
-        halves(before), (proj_hi[pl.ds(0, top), :], proj_lo[pl.ds(0, top), :]), NT)
-    add = dot3(halves(jnp.concatenate([above, below], axis=1)), (proj_hi[...], proj_lo[...]), NN)
-    upper_out[...] = add.reshape(chunks, rows, half)
-    each(both(tail, no(head)), lambda c: local_b(c).start())
-    solved_tail[...] = below.reshape(chunks, rows, half)
-    top_rows[...] = above.reshape(chunks, rows, top)
+        prepare()
+
+    def step(c):
+        group_f(c).wait_recv()
+        pass_on_f(c)
+    each(both(no(start_group), no(end_group), no(tail)), step)
+
+    @pl.when(both(no(start_group), no(end_group)))
+    def _():
+        add = dot_stacked(enter_f[...].reshape(traits, half), enter_add_w[...])
+        upper_out[...] += add.reshape(chunks, rows, half)
+
+    each(both(tail, no(head), no(end_group)), lambda c: local_b(c).start())
 
     def step(c):
         local_b(c).wait_recv()
@@ -238,13 +289,49 @@
         @pl.when(no(head))
         def _():
             local_b(c).start()
-
-        @pl.when(both(head, end_group, no(start_group)))
+    each(both(no(tail), no(end_group)), step)
+
+    def step(c):
+        @pl.when(no(start_group))
+        def _():
+            group_f(c).wait_recv()
+            pass_on_f(c)
+            upper_out[c] = upper_out[c] + dot_stacked(enter_f[c], enter_add_w[...])
+
+        @pl.when(no(tail))
+        def _():
+            local_b(c).wait_recv()
+            upper_out[c] = upper_out[c] + dot_stacked(upper_in[c], backward_w[...])
+
+        @pl.when(no(head))
+        def _():
+            local_b(c).start()
+
+        @pl.when(both(head, no(start_group)))
         def _():
             group_b(c).start()
-    each(no(tail), step)
-    if group == 1:
-        each(both(end_group, no(start_group)), lambda c: group_b(c).start())
+    each(end_group, step)
+
+    all_rows = jnp.concatenate([top_rows[...].reshape(traits, top),
+                                tail_out[...].reshape(traits, half)], axis=1)
+    base[...] = all_rows
+
+    @pl.when(no(start_group))
+    def _():
+        base[...] += dot_stacked(enter_f[...].reshape(traits, half), enter_rows_w[...])
+
+    base[:, top:] -= upper_in[...].reshape(traits, half)
+    base[...] = dot3(halves(base[...]), (inv_hi[...], inv_lo[...]), NN)
+
+    @pl.when(no(end_group))
+    def _():
+        slope = dot3(halves(map_b_in[...].reshape(half, half)),
+                     (inv_hi[pl.ds(top, half), :], inv_lo[pl.ds(top, half), :]), NN)
+        enter_base_w[...] = stacked(halves(slope))
+
+    @pl.when(g < count // 2)
+    def _():
+        make_mask()
 
     @pl.when(both(no(end_group), head))
     def _():
@@ -252,9 +339,7 @@
 
         def go(c, _):
             group_b(c).wait_recv()
-
-            if group > 1:
-                pass_b(c).start()
+            pass_on_b(c)
 
             @pl.when(no(start_group))
             def _():
@@ -263,23 +348,16 @@
             return 0
         lax.fori_loop(0, chunks, go, 0)
 
-    @pl.when(g < count // 2)
-    def _():
-        make_mask()
-
-    def step(c):
-        pass_b(c).wait_recv()
-
-        @pl.when(no(tail))
-        def _():
-            pass_b(c).start()
+    def step(c):
+        group_b(c).wait_recv()
+        pass_on_b(c)
     each(both(no(end_group), no(head)), step)
 
-    after = upper_in[...].reshape(traits, half) + dot_stacked(
-        enter_b[...].reshape(traits, half), stacked(halves(map_b_in[...].reshape(half, half))))
-    rows_now = jnp.concatenate(
-        [top_rows[...].reshape(traits, top), solved_tail[...].reshape(traits, half) - after], axis=1)
-    weights = dot3(halves(rows_now), (inv_hi[...], inv_lo[...]), NN).astype(BF16)
+    @pl.when(no(end_group))
+    def _():
+        base[...] -= dot_stacked(enter_b[...].reshape(traits, half), enter_base_w[...])
+
+    weights = base[...].astype(BF16)
     left_out[...] = weights[:, top:]
     right_out[...] = weights[:, :half]
 
@@ -308,11 +386,13 @@
     each(both(no(start_group), no(tail)), lambda c: map_f(c).wait_send())
     each(no(tail), lambda c: local_f(c).wait_send())
     each(both(tail, no(end_group)), lambda c: group_f(c).wait_send())
-    each(both(no(head), no(start_group)), lambda c: pass_f(c).wait_send())
+    each(both(no(even), no(start_group)), lambda c: pass_f(c).wait_send())
+    each(both(no(even), q >= 2, no(start_group)), lambda c: pass_f_two(c).wait_send())
     each(both(no(end_group), no(head)), lambda c: map_b(c).wait_send())
     each(no(head), lambda c: local_b(c).wait_send())
     each(both(head, no(start_group)), lambda c: group_b(c).wait_send())
-    each(both(no(tail), no(end_group)), lambda c: pass_b(c).wait_send())
+    each(both(even, q + 1 < group, no(end_group)), lambda c: pass_b(c).wait_send())
+    each(both(even, q + 2 < group, no(end_group)), lambda c: pass_b_two(c).wait_send())
 
     @pl.when(no(last))
     def _():
@@ -339,21 +419,26 @@
     return pl.pallas_call(
         functools.partial(kernel, n, group),
         out_shape=jax.ShapeDtypeStruct((traits, units), F32),
-        in_specs=[pl.BlockSpec(memory_space=pltpu.VMEM)] * 5,
+        in_specs=[pl.BlockSpec(memory_space=pltpu.HBM)] * 5,
         out_specs=pl.BlockSpec(memory_space=pltpu.VMEM),
         scratch_shapes=[
+            pltpu.VMEM((traits, typed), F32), pltpu.VMEM((typed, typed), F32),
+            pltpu.VMEM((typed, half), F32), pltpu.VMEM((units, span), BF16),
+            pltpu.VMEM((1, units), jnp.int32), pltpu.SemaphoreType.DMA((5,)),
             state, state, state, state, state, state, state,
             chain_map, chain_map, chain_map, chain_map, edge, edge, edge, edge,
-            pltpu.VMEM((chunks, rows, top), F32),
+            pltpu.VMEM((chunks, rows, top), F32), pltpu.VMEM((traits, typed), F32),
+            pltpu.VMEM((3 * half, typed), BF16), pltpu.VMEM((3 * half, half), BF16),
+            pltpu.VMEM((3 * half, typed), BF16),
             pltpu.VMEM((3 * half, half), BF16), pltpu.VMEM((3 * half, half), BF16),
             pltpu.VMEM((typed, typed), BF16), pltpu.VMEM((typed, typed), BF16),
             pltpu.VMEM((typed, half), BF16), pltpu.VMEM((typed, half), BF16),
             pltpu.VMEM((units, span), BF16),
-            pltpu.SemaphoreType.DMA((8, chunks)), pltpu.SemaphoreType.DMA((6, chunks)),
+            pltpu.SemaphoreType.DMA((10, chunks)), pltpu.SemaphoreType.DMA((6, chunks)),
             pltpu.SemaphoreType.DMA((2,)), pltpu.SemaphoreType.DMA((2,)),
         ],
         compiler_params=pltpu.CompilerParams(
-            collective_id=0, has_side_effects=True, vmem_limit_bytes=48 * 1024 * 1024),
+            collective_id=0, has_side_effects=True, vmem_limit_bytes=63 * 1024 * 1024),
     )(z_typed, diag_inverse[0], coupling[0], impute_coef, anchor.reshape(1, units))
 
 

time: 57.3 us -> 53.3 us (0.930)
  local copies, waits for them, and re-layouts: 6.01 us -> 1.87 us
    unnamed x11 -> x1, local copies, waits for them, and re-layouts: 6.01 us -> 1.87 us
where the time goes in v3:
time: 53.3 us; the launch traced here: 53.1 us
  Pallas kernels  51.2 us (96%)
  local copies, waits for them, and re-layouts  1.87 us (4%)
    pallas_call x1, Pallas kernels, per_device(): pl.pallas_call(functools.partial(kernel, n, group), out_shape=jax.ShapeDt...  51.2 us
    unnamed x1, local copies, waits for them, and re-layouts  1.87 us

profile of v3, /device:TPU:1, one launch (start us, length us, event | category | flops | bytes accessed | tf_op | source)
XLA Modules:
  0.0 53.1 jit_solution(16338046027504254100)
XLA Ops:
  0.0 51.2 %shard_map.55 = f32[256,512]{1,0:T(8,128)} custom-call(f32[256,512]{1,0:T(8,128)} %z_hbm.1, f32[512,512]{1,0:T(8,128)} %bitcast.3, f32[512,256]{1,0:T(8,128)} %bitcast.4, bf16[512,1024]{1,0:T(8,128)(2,1)} %coef_hbm.1, s32[1,512]{1,0:T(1,128)} %bitcast.5), custom_call_target="tpu_custom_call" | custom-call | tf_op jit(solution)/shard_map/pallas_call | solution.py:419
  51.3 1.9 %copy.7 = f32[256,512]{1,0:T(8,128)} copy(f32[256,512]{1,0:T(8,128)} %shard_map.55) | data formatting | bytes 1048576

commit v4 on v3

--- a/solution.py
+++ b/solution.py
@@ -163,8 +163,8 @@
 
     def start_head(c):
         map_f(c).start()
+        local_f(c).start()
     each(both(head, no(start_group), no(tail)), start_head)
-    each(both(head, no(start_group), no(tail)), lambda c: local_f(c).start())
     each(both(tail, no(end_group), no(head)), lambda c: map_b(c).start())
 
     clear(head, tail_in)
@@ -178,11 +178,15 @@
 
     def step(c):
         map_f(c).wait_recv()
-        map_f_out[c] = dot_stacked(map_f_in[c], forward_w[...])
+        local_f(c).wait_recv()
+        moved = dot_stacked(jnp.concatenate([map_f_in[c], tail_in[c]], axis=0), forward_w[...])
+        map_f_out[c] = moved[:half // chunks]
+        tail_out[c] = tail_out[c] + moved[half // chunks:]
 
         @pl.when(no(tail))
         def _():
             map_f(c).start()
+            local_f(c).start()
     each(both(no(start_group), no(head)), step)
 
     def step(c):
@@ -197,7 +201,7 @@
         def _():
             carry_f[c] = tail_out[c]
             group_f(c).start()
-    each(no(head), step)
+    each(both(start_group, no(head)), step)
     if group == 1:
         def step(c):
             carry_f[c] = tail_out[c]
@@ -333,6 +337,19 @@
     def _():
         make_mask()
 
+    def drain_early():
+        each(both(no(start_group), no(tail)), lambda c: map_f(c).wait_send())
+        each(no(tail), lambda c: local_f(c).wait_send())
+        each(both(tail, no(end_group)), lambda c: group_f(c).wait_send())
+        each(both(no(even), no(start_group)), lambda c: pass_f(c).wait_send())
+        each(both(no(even), q >= 2, no(start_group)), lambda c: pass_f_two(c).wait_send())
+        each(both(no(end_group), no(head)), lambda c: map_b(c).wait_send())
+        each(no(head), lambda c: local_b(c).wait_send())
+
+    @pl.when(g < count // 2)
+    def _():
+        drain_early()
+
     @pl.when(both(no(end_group), head))
     def _():
         whole = stacked(halves(map_b_out[...].reshape(half, half)))
@@ -383,13 +400,10 @@
 
     out_ref[...] += product(left_in[...], masked[:, :half], NT)
 
-    each(both(no(start_group), no(tail)), lambda c: map_f(c).wait_send())
-    each(no(tail), lambda c: local_f(c).wait_send())
-    each(both(tail, no(end_group)), lambda c: group_f(c).wait_send())
-    each(both(no(even), no(start_group)), lambda c: pass_f(c).wait_send())
-    each(both(no(even), q >= 2, no(start_group)), lambda c: pass_f_two(c).wait_send())
-    each(both(no(end_group), no(head)), lambda c: map_b(c).wait_send())
-    each(no(head), lambda c: local_b(c).wait_send())
+    @pl.when(g >= count // 2)
+    def _():
+        drain_early()
+
     each(both(head, no(start_group)), lambda c: group_b(c).wait_send())
     each(both(even, q + 1 < group, no(end_group)), lambda c: pass_b(c).wait_send())
     each(both(even, q + 2 < group, no(end_group)), lambda c: pass_b_two(c).wait_send())

time: 53.3 us -> 53.2 us (level)
  no operation moved by 1% of the time
where the time goes in v4:
time: 53.2 us; the launch traced here: 53.1 us
  Pallas kernels  51.2 us (96%)
  local copies, waits for them, and re-layouts  1.87 us (4%)
    pallas_call x1, Pallas kernels, per_device(): pl.pallas_call(functools.partial(kernel, n, group), out_shape=jax.ShapeDt...  51.2 us
    unnamed x1, local copies, waits for them, and re-layouts  1.87 us

profile of v4, /device:TPU:1, one launch (start us, length us, event | category | flops | bytes accessed | tf_op | source)
XLA Modules:
  0.0 53.1 jit_solution(12987364742694818675)
XLA Ops:
  0.0 51.2 %shard_map.55 = f32[256,512]{1,0:T(8,128)} custom-call(f32[256,512]{1,0:T(8,128)} %z_hbm.1, f32[512,512]{1,0:T(8,128)} %bitcast.3, f32[512,256]{1,0:T(8,128)} %bitcast.4, bf16[512,1024]{1,0:T(8,128)(2,1)} %coef_hbm.1, s32[1,512]{1,0:T(1,128)} %bitcast.5), custom_call_target="tpu_custom_call" | custom-call | tf_op jit(solution)/shard_map/pallas_call | solution.py:433
  51.2 1.9 %copy.7 = f32[256,512]{1,0:T(8,128)} copy(f32[256,512]{1,0:T(8,128)} %shard_map.55) | data formatting | bytes 1048576

commit v5 on v4

--- a/solution.py
+++ b/solution.py
@@ -41,6 +41,7 @@
     tail_in, tail_out, upper_in, upper_out, enter_f, enter_b, carry_f,
     map_f_in, map_f_out, map_b_in, map_b_out, left_in, right_in, left_out, right_out,
     top_rows, base, enter_rows_w, enter_add_w, enter_base_w, forward_w, backward_w, inv_hi, inv_lo, proj_hi, proj_lo, masked,
+    pre_base_out, pre_base_in, pre_slope_out, pre_slope_in, ps, pr,
     sent, got, es, er,
 ):
     me = lax.axis_index("genome")
@@ -117,6 +118,11 @@
     def to_left():
         return remote(right_out, right_in, es.at[1], er.at[1], left)
 
+    def ahead(side):
+        other = (right, left)[side]
+        return (remote(pre_base_out.at[side], pre_base_in.at[side], ps.at[side, 0], pr.at[side, 0], other),
+                remote(pre_slope_out.at[side], pre_slope_in.at[side], ps.at[side, 1], pr.at[side, 1], other))
+
     def each(condition, step):
         @pl.when(condition)
         def _():
@@ -332,6 +338,17 @@
         slope = dot3(halves(map_b_in[...].reshape(half, half)),
                      (inv_hi[pl.ds(top, half), :], inv_lo[pl.ds(top, half), :]), NN)
         enter_base_w[...] = stacked(halves(slope))
+        pre_base_out[0] = base[:, top:]
+        pre_slope_out[0] = slope[:, top:]
+        pre_base_out[1] = base[:, :half]
+        pre_slope_out[1] = slope[:, :half]
+        for copy in ahead(0):
+            copy.start()
+
+        @pl.when(no(head))
+        def _():
+            for copy in ahead(1):
+                copy.start()
 
     @pl.when(g < count // 2)
     def _():
@@ -378,23 +395,44 @@
     left_out[...] = weights[:, top:]
     right_out[...] = weights[:, :half]
 
-    @pl.when(no(last))
+    late_right = both(end_group, no(last))
+    late_left = both(no(first), jnp.logical_or(head, end_group))
+
+    @pl.when(late_right)
     def _():
         to_right().start()
 
-    @pl.when(no(first))
+    @pl.when(late_left)
     def _():
         to_left().start()
 
+    def edge(side, state):
+        for copy in ahead(side):
+            copy.wait_recv()
+        return (pre_base_in[side] - dot_stacked(
+            state.reshape(traits, half), stacked(halves(pre_slope_in[side])))).astype(BF16)
+
+    @pl.when(both(no(end_group), no(head)))
+    def _():
+        left_in[...] = edge(0, enter_b[...])
+
+    @pl.when(both(head, no(start_group)))
+    def _():
+        left_in[...] = edge(0, upper_out[...])
+
+    @pl.when(both(no(end_group), no(tail)))
+    def _():
+        right_in[...] = edge(1, enter_b[...])
+
     out_ref[...] = product(weights, masked[:, half:half + typed], NT)
 
-    @pl.when(no(last))
+    @pl.when(both(no(last), jnp.logical_or(tail, end_group)))
     def _():
         to_left().wait_recv()
 
     out_ref[...] += product(right_in[...], masked[:, half + typed:], NT)
 
-    @pl.when(no(first))
+    @pl.when(both(end_group, no(head)))
     def _():
         to_right().wait_recv()
 
@@ -408,13 +446,23 @@
     each(both(even, q + 1 < group, no(end_group)), lambda c: pass_b(c).wait_send())
     each(both(even, q + 2 < group, no(end_group)), lambda c: pass_b_two(c).wait_send())
 
-    @pl.when(no(last))
+    @pl.when(late_right)
     def _():
         to_right().wait_send()
 
-    @pl.when(no(first))
+    @pl.when(late_left)
     def _():
         to_left().wait_send()
+
+    @pl.when(no(end_group))
+    def _():
+        for copy in ahead(0):
+            copy.wait_send()
+
+    @pl.when(both(no(end_group), no(head)))
+    def _():
+        for copy in ahead(1):
+            copy.wait_send()
 
 
 def per_device(n, z_typed, diag_inverse, coupling, impute_coef, anchor):
@@ -448,6 +496,9 @@
             pltpu.VMEM((typed, typed), BF16), pltpu.VMEM((typed, typed), BF16),
             pltpu.VMEM((typed, half), BF16), pltpu.VMEM((typed, half), BF16),
             pltpu.VMEM((units, span), BF16),
+            pltpu.VMEM((2, traits, half), F32), pltpu.VMEM((2, traits, half), F32),
+            pltpu.VMEM((2, half, half), F32), pltpu.VMEM((2, half, half), F32),
+            pltpu.SemaphoreType.DMA((2, 2)), pltpu.SemaphoreType.DMA((2, 2)),
             pltpu.SemaphoreType.DMA((10, chunks)), pltpu.SemaphoreType.DMA((6, chunks)),
             pltpu.SemaphoreType.DMA((2,)), pltpu.SemaphoreType.DMA((2,)),
         ],

time: 53.2 us -> 52 us (0.977)
  the two profiles are of different devices: /device:TPU:1 before, /device:TPU:7 now
where the time goes in v5:
time: 52 us; the launch traced here: 51.8 us
  Pallas kernels  49.9 us (96%)
  local copies, waits for them, and re-layouts  1.87 us (4%)
    pallas_call x1, Pallas kernels, per_device(): pl.pallas_call(functools.partial(kernel, n, group), out_shape=jax.ShapeDt...  49.9 us
    unnamed x1, local copies, waits for them, and re-layouts  1.87 us

profile of v5, /device:TPU:7, one launch (start us, length us, event | category | flops | bytes accessed | tf_op | source)
XLA Modules:
  0.0 51.8 jit_solution(14190652203182251492)
XLA Ops:
  0.0 49.9 %shard_map.55 = f32[256,512]{1,0:T(8,128)} custom-call(f32[256,512]{1,0:T(8,128)} %z_hbm.1, f32[512,512]{1,0:T(8,128)} %bitcast.3, f32[512,256]{1,0:T(8,128)} %bitcast.4, bf16[512,1024]{1,0:T(8,128)(2,1)} %coef_hbm.1, s32[1,512]{1,0:T(1,128)} %bitcast.5), custom_call_target="tpu_custom_call" | custom-call | tf_op jit(solution)/shard_map/pallas_call | solution.py:481
  49.9 1.9 %copy.7 = f32[256,512]{1,0:T(8,128)} copy(f32[256,512]{1,0:T(8,128)} %shard_map.55) | data formatting | bytes 1048576

commit v6 on v5

--- a/solution.py
+++ b/solution.py
@@ -123,6 +123,8 @@
         return (remote(pre_base_out.at[side], pre_base_in.at[side], ps.at[side, 0], pr.at[side, 0], other),
                 remote(pre_slope_out.at[side], pre_slope_in.at[side], ps.at[side, 1], pr.at[side, 1], other))
 
+    early_right = both(no(end_group), no(both(tail, g == count - 2)))
+
     def each(condition, step):
         @pl.when(condition)
         def _():
@@ -342,8 +344,10 @@
         pre_slope_out[0] = slope[:, top:]
         pre_base_out[1] = base[:, :half]
         pre_slope_out[1] = slope[:, :half]
-        for copy in ahead(0):
-            copy.start()
+        @pl.when(early_right)
+        def _():
+            for copy in ahead(0):
+                copy.start()
 
         @pl.when(no(head))
         def _():
@@ -395,7 +399,7 @@
     left_out[...] = weights[:, top:]
     right_out[...] = weights[:, :half]
 
-    late_right = both(end_group, no(last))
+    late_right = both(no(last), no(early_right))
     late_left = both(no(first), jnp.logical_or(head, end_group))
 
     @pl.when(late_right)
@@ -416,7 +420,7 @@
     def _():
         left_in[...] = edge(0, enter_b[...])
 
-    @pl.when(both(head, no(start_group)))
+    @pl.when(both(head, no(start_group), no(end_group)))
     def _():
         left_in[...] = edge(0, upper_out[...])
 
@@ -432,7 +436,7 @@
 
     out_ref[...] += product(right_in[...], masked[:, half + typed:], NT)
 
-    @pl.when(both(end_group, no(head)))
+    @pl.when(both(end_group, no(first)))
     def _():
         to_right().wait_recv()
 
@@ -454,7 +458,7 @@
     def _():
         to_left().wait_send()
 
-    @pl.when(no(end_group))
+    @pl.when(early_right)
     def _():
         for copy in ahead(0):
             copy.wait_send()

time: 52 us -> 52.3 us (level)
  no operation moved by 1% of the time
where the time goes in v6:
time: 52.3 us; the launch traced here: 52.1 us
  Pallas kernels  50.2 us (96%)
  local copies, waits for them, and re-layouts  1.87 us (4%)
    pallas_call x1, Pallas kernels, per_device(): pl.pallas_call(functools.partial(kernel, n, group), out_shape=jax.ShapeDt...  50.2 us
    unnamed x1, local copies, waits for them, and re-layouts  1.87 us

profile of v6, /device:TPU:7, one launch (start us, length us, event | category | flops | bytes accessed | tf_op | source)
XLA Modules:
  0.0 52.1 jit_solution(11488354797814344233)
XLA Ops:
  0.0 50.2 %shard_map.55 = f32[256,512]{1,0:T(8,128)} custom-call(f32[256,512]{1,0:T(8,128)} %z_hbm.1, f32[512,512]{1,0:T(8,128)} %bitcast.3, f32[512,256]{1,0:T(8,128)} %bitcast.4, bf16[512,1024]{1,0:T(8,128)(2,1)} %coef_hbm.1, s32[1,512]{1,0:T(1,128)} %bitcast.5), custom_call_target="tpu_custom_call" | custom-call | tf_op jit(solution)/shard_map/pallas_call | solution.py:485
  50.2 1.9 %copy.7 = f32[256,512]{1,0:T(8,128)} copy(f32[256,512]{1,0:T(8,128)} %shard_map.55) | data formatting | bytes 1048576
